TPU v7x, 256 devices: a whole 4x4x8 slice. The times are simulated.
256 devices in a mesh: ctx: 64 (over x_hi, z, y), head: 4 (over x_lo, core).
Axes of the slice: x: 4 (x_hi: 2, x_lo: 2; x = x_hi * 2 + x_lo), y: 4, z: 8, core: 2. Of those that a mesh axis runs over, the one named last changes fastest.
Arguments:
- queries: bfloat16 [8192, 4096], P('ctx', 'head'), may hold values from -81 to 81
- key_states: bfloat16 [8192, 1024], P('ctx', 'head'), may hold values from -7 to 7
- value_states: bfloat16 [8192, 1024], P('ctx', 'head'), may hold values from -6 to 6
- out_weight: bfloat16 [4096, 4096], P('head'), may hold values from -0.09375 to 0.09375
- head_role: int32 [8], replicated, may hold values from 0 to 1, as said below
- sink_len: int32 [8], replicated, may hold values from 32 to 128, as said below
- window_len: int32 [8], replicated, may hold values from 256 to 1024, as said below
Outputs:
- mixed: bfloat16 [8192, 4096], P(('ctx', 'head'))
Inputs may be any that keep to these rules, and one draw needn't show every extreme that they name: `head_role`: exactly 4 heads are retrieval heads. `sink_len`: some head has exactly 128. `window_len`: some head has exactly 1024.
All inputs are finite; a program needn't handle non-finite values.
Results may differ from a plain program's by a relative error of at most 0.012.
Values may be sent and summed in bfloat16 or wider, within the bound.
A program may use at most 128 MiB of HBM per device.

v0:
```python
import jax
import jax.numpy as jnp
from jax import lax
from jax.sharding import PartitionSpec as P

HD = 128
GROUP = 4
NEGATIVE = -1e30


def online_update(running, query_heads, key_part, value_part, allowed):
    row_peak, row_total, weighted = running
    scores = jnp.einsum(
        "thgd,jhd->thgj", query_heads, key_part, preferred_element_type=jnp.float32
    ) * HD ** (-0.5)
    visible = allowed[:, :, None, :]
    block_peak = jnp.max(jnp.where(visible, scores, NEGATIVE), axis=-1)
    new_peak = jnp.maximum(row_peak, block_peak)
    weights = jnp.where(visible, jnp.exp(scores - new_peak[..., None]), 0.0)
    row_total = jnp.sum(weights, axis=-1)
    weighted = jnp.einsum(
        "thgj,jhd->thgd",
        weights.astype(jnp.bfloat16),
        value_part,
        preferred_element_type=jnp.float32,
    )
    return (new_peak, row_total, weighted)


def empty_state(row_count, head_count):
    return (
        jnp.full((row_count, head_count, GROUP), NEGATIVE, jnp.float32),
        jnp.zeros((row_count, head_count, GROUP), jnp.float32),
        jnp.zeros((row_count, head_count, GROUP, HD), jnp.float32),
    )


def finish(running, row_count):
    row_peak, row_total, weighted = running
    return (weighted / row_total[..., None]).astype(jnp.bfloat16).reshape(row_count, -1)


def per_device(queries, key_states, value_states, out_weight, head_role, sink_len, window_len):
    row_count = queries.shape[0]
    local_heads = key_states.shape[1] // HD
    row_base = lax.axis_index("ctx") * row_count
    query_pos = row_base + jnp.arange(row_count, dtype=jnp.int32)
    my_group = lax.axis_index("head")
    first_head = my_group * local_heads
    last_row = row_base + row_count - 1
    roles_here = lax.dynamic_slice_in_dim(head_role, first_head, local_heads)
    sinks_here = lax.dynamic_slice_in_dim(sink_len, first_head, local_heads)
    windows_here = lax.dynamic_slice_in_dim(window_len, first_head, local_heads)
    query_heads = queries.reshape(row_count, local_heads, GROUP, HD)
    key_part = lax.all_gather(key_states, "ctx", axis=0, tiled=True).reshape(-1, local_heads, HD)
    value_part = lax.all_gather(value_states, "ctx", axis=0, tiled=True).reshape(
        -1, local_heads, HD
    )
    key_pos = jnp.arange(key_part.shape[0], dtype=jnp.int32)

    def update(state):
        later = query_pos[:, None, None]
        earlier = key_pos[None, None, :]
        allowed = (earlier <= later) & (
            (roles_here[None, :, None] == 1)
            | (earlier < sinks_here[None, :, None])
            | (later - earlier < windows_here[None, :, None])
        )
        return online_update(state, query_heads, key_part, value_part, allowed)

    def unchanged(state):
        return state

    running = lax.cond(
        jnp.int32(0) <= last_row, update, unchanged, empty_state(row_count, local_heads)
    )
    attended = finish(running, row_count)
    mixed = lax.psum_scatter(
        jnp.dot(attended, out_weight, preferred_element_type=jnp.float32).astype(jnp.bfloat16),
        "head",
        scatter_dimension=0,
        tiled=True,
    )
    return mixed


def solution(mesh):
    in_specs = (
        P("ctx", "head"),
        P("ctx", "head"),
        P("ctx", "head"),
        P("head", None),
        P(),
        P(),
        P(),
    )
    out_specs = P(("ctx", "head"), None)
    return jax.shard_map(
        per_device, mesh=mesh, in_specs=in_specs, out_specs=out_specs, check_vma=False
    )
```

profile of v0, /device:TPU:1, one launch (start us, length us, event | category | flops | bytes accessed | tf_op | source)
XLA Modules:
  0.0 373.8 jit_solution(10370154354749702863)
XLA Ops:
  6.5 0.0 all-gather.3.cloned.1.call-start
  6.5 0.7 all-gather.3.cloned.1.call-update
  7.3 0.0 all-gather.5.cloned.1.call-start
  7.3 0.7 all-gather.5.cloned.1.call-update
  8.0 0.0 reduce-scatter.2.cloned.1.call-start
  8.1 131.3 %all-gather.3.cloned.1.call-done = bf16[8192,256]{1,0:T(8,128)(2,1)} async-done(((bf16[128,256]{1,0:T(8,128)(2,1)}), bf16[8192,256]{1,0:T(8,128)(2,1)}) %all-gather.3.cloned.1.call-update) | async-done | bytes 4194320 | tf_op jit(solution)/shard_map/all_gather | solution.py:55
  139.4 128.3 %all-gather.5.cloned.1.call-done = bf16[8192,256]{1,0:T(8,128)(2,1)} async-done(((bf16[128,256]{1,0:T(8,128)(2,1)}), bf16[8192,256]{1,0:T(8,128)(2,1)}) %all-gather.5.cloned.1.call-update) | async-done | bytes 4194320 | tf_op jit(solution)/shard_map/all_gather | solution.py:56
  267.6 70.6 %conditional.1 = (f32[128,2,4]{0,2,1:T(4,128)S(1)}, f32[128,2,4,128]{0,3,2,1:T(8,128)S(1)}) conditional(s32[]{:T(128)} %convert_element_type.15, () %tuple.22, (s32[8192]{0:T(1024)S(1)}, s32[8192]{0:T(1024)S(1)}, s32[]{:T(128)}, s32[128]{0:T(128)S(1)}, s32[]{:T(128)}, /*index=5*/s32[8]{0:T(128)}, s32[8192]{0:T(1024)S(1)}, s32[8]{0:T(128)}, ...), branch_computations={%region_0.0_spmd, %region_1.4_spmd} | conditional | flops 4395662336 | bytes 148269232 | solution.py:74
  267.6 0.7 dynamic-slice_compare_fusion
  268.4 0.7 dynamic_slice.19
  269.1 0.1 compare_or_fusion
  269.2 0.7 dynamic_slice.20
  269.9 1.2 broadcast_subtract_fusion
  271.2 0.0 copy-start
  271.2 3.7 broadcast_compare_fusion
  274.9 2.8 or_and_fusion
  277.7 6.9 %reshape.125 = bf16[8192,2,128]{2,1,0:T(2,128)(2,1)} reshape(bf16[8192,256]{1,0:T(8,128)(2,1)} %get-tuple-element.125) | data formatting | bytes 8388608 | tf_op jit(solution)/shard_map/reshape | solution.py:55
  284.6 0.0 copy-done
  284.6 0.2 reshape.126
  284.8 15.7 %fusion = (f32[128,2,4]{0,2,1:T(4,128)S(1)}, f32[2,8192,128,4]{2,1,3,0:T(8,128)}) fusion(pred[128,2,8192]{0,2,1:T(8,128)(4,1)S(1)} %or_and_fusion, bf16[128,2,4,128]{3,2,1,0:T(4,128)(2,1)S(1)} %reshape.126, bf16[8192,2,128,1]{2,1,0,3:T(2,128)(2,1)} %bitcast.23), kind=kOutput, calls=%fused_computation.2 | convolution fusion | flops 2172648448 | bytes 40112128 | tf_op jit(solution)/shard_map/cond/branch_1_fun/thgd,jhd->thgj/dot_general | solution.py:13
  300.5 6.9 %reshape.127 = bf16[8192,2,128]{2,1,0:T(2,128)(2,1)} reshape(bf16[8192,256]{1,0:T(8,128)(2,1)} %get-tuple-element.127) | data formatting | bytes 8388608 | tf_op jit(solution)/shard_map/reshape | solution.py:56
  307.4 16.3 %fusion.11 = f32[128,2,4,128]{3,0,2,1:T(8,128)S(1)} fusion(bf16[8192,2,128,1]{2,1,0,3:T(2,128)(2,1)} %bitcast.24, f32[2,8192,128,4]{2,1,3,0:T(8,128)} %get-tuple-element.142, f32[128,2,4]{0,2,1:T(4,128)S(1)} %broadcast_maximum_fusion, pred[128,2,8192]{0,2,1:T(8,128)(4,1)S(1)} %or_and_fusion), kind=kOutput, calls=%fused_computation.15 | convolution fusion | flops 2181038080 | bytes 40374272 | tf_op jit(solution)/shard_map/cond/branch_1_fun/thgj,jhd->thgd/dot_general | solution.py:21
  323.7 0.2 copy.36
  323.9 14.3 %fusion.4 = f32[128,2,4]{0,2,1:T(4,128)S(1)} fusion(f32[2,8192,128,4]{2,1,3,0:T(8,128)} %get-tuple-element.142, f32[128,2,4]{0,2,1:T(4,128)S(1)} %broadcast_maximum_fusion, pred[128,2,8192]{0,2,1:T(8,128)(4,1)S(1)} %or_and_fusion), kind=kLoop, calls=%fused_computation.6 | loop fusion | flops 33553408 | bytes 35659776 | tf_op jit(solution)/shard_map/cond/branch_1_fun/reduce_sum | solution.py:20
  338.3 0.1 divide_convert_fusion
  338.3 5.6 %convolution_convert_fusion = bf16[128,4096]{1,0:T(8,128)(2,1)} fusion(bf16[128,1024]{0,1:T(8,128)(2,1)S(1)} %bitcast.25, bf16[1024,4096]{1,0:T(8,128)(2,1)} %param.12), kind=kOutput, calls=%fused_computation.23 | convolution fusion | flops 1074266112 | bytes 9699328 | tf_op jit(solution)/shard_map/dot_general | solution.py:79
  344.0 0.0 reduce-scatter.2.cloned.1.call-update
  344.0 23.3 %reduce-scatter.2.cloned.1.call-done = bf16[32,4096]{1,0:T(8,128)(2,1)} async-done(((bf16[128,4096]{1,0:T(8,128)(2,1)}), bf16[32,4096]{1,0:T(8,128)(2,1)}) %reduce-scatter.2.cloned.1.call-update) | async-done | bytes 262160 | tf_op jit(solution)/shard_map/reduce_scatter | solution.py:78
  (4 shorter events, 0.0 us)
Async XLA Ops:
  6.5 132.8 %all-gather.3.cloned.1.call-start = ((), (), s32[]{:S(2)}) async-start(), calls=%async_computation.1 | async-start | bytes 4259840 | tf_op jit(solution)/shard_map/all_gather | solution.py:55
  7.3 260.4 %all-gather.5.cloned.1.call-start = ((), (), s32[]{:S(2)}) async-start(), calls=%async_computation.2 | async-start | bytes 4259840 | tf_op jit(solution)/shard_map/all_gather | solution.py:56
  8.0 359.3 %reduce-scatter.2.cloned.1.call-start = ((), (), s32[]{:S(2)}) async-start(), calls=%async_computation.3 | async-start | bytes 1310720 | tf_op jit(solution)/shard_map/reduce_scatter | solution.py:78
  271.2 13.4 %copy-start = (bf16[128,1024]{1,0:T(8,128)(2,1)S(1)}, bf16[128,1024]{1,0:T(8,128)(2,1)}, u32[]{:S(2)}) copy-start(bf16[128,1024]{1,0:T(8,128)(2,1)} %get-tuple-element.139) | copy-start | bytes 786436 | tf_op jit(solution)/shard_map/cond
Sparse Core Ops, SparseCore 0:
  10.9 128.4 all-gather.2
  142.9 124.6 all-gather.4
  344.1 23.1 reduce-scatter.1
where the time goes:
time: 374 us
  waiting for transfers between devices  284 us (76%)
  matrix products  37.7 us (10%)
  other arithmetic  23 us (6%)
  local copies, waits for them, and re-layouts  15.6 us (4%)
  between operations  13.1 us (4%)
    all_gather x1, waiting for transfers between devices, per_device(): lax.all_gather(key_states, 'ctx', axis=0, tiled=True)  131 us
    all_gather x1, waiting for transfers between devices, per_device(): lax.all_gather(value_states, 'ctx', axis=0, tiled=True)  128 us
    reduce_scatter x1, waiting for transfers between devices, per_device(): lax.psum_scatter(jnp.dot(attended, out_weight, preferred_element_type=jnp...  23.3 us
    dot_general x1, matrix products, online_update(): jnp.einsum('thgj,jhd->thgd', weights.astype(jnp.bfloat16), value_part, pr...  16.3 us
    dot_general x1, matrix products, online_update(): jnp.einsum('thgd,jhd->thgj', query_heads, key_part, preferred_element_typ...  15.7 us
    reduce_sum x1, other arithmetic, online_update(): row_total = jnp.sum(weights, axis=-1)  14.3 us
  transfers between devices with their start and end apart: 3, of which 3 were waited for; matrix products, arithmetic and copies ran while one was open for 0% of the time, Pallas kernels for 0%

commit v1 on v0

--- a/solution.py
+++ b/solution.py
@@ -52,7 +52,9 @@
     sinks_here = lax.dynamic_slice_in_dim(sink_len, first_head, local_heads)
     windows_here = lax.dynamic_slice_in_dim(window_len, first_head, local_heads)
     query_heads = queries.reshape(row_count, local_heads, GROUP, HD)
-    key_part = lax.all_gather(key_states, "ctx", axis=0, tiled=True).reshape(-1, local_heads, HD)
+    key_part = jnp.concatenate(
+        lax.all_to_all(jnp.stack([key_states] * lax.axis_size("ctx")), "ctx", 0, 0), axis=0
+    ).reshape(-1, local_heads, HD)
     value_part = lax.all_gather(value_states, "ctx", axis=0, tiled=True).reshape(
         -1, local_heads, HD
     )

time: 374 us -> 275 us (0.74)
  waiting for transfers between devices: 284 us -> 167 us
  starting transfers between devices: 0.08 us -> 15.5 us
    all_gather x1 -> x0, waiting for transfers between devices: 131 us -> none  [per_device(): lax.all_gather(key_states, 'ctx', axis=0, tiled=True)]
    all_to_all x0 -> x1, waiting for transfers between devices: none -> 99.9 us  [per_device(): lax.all_to_all(jnp.stack([key_states] * lax.axis_size('ctx')), 'ctx', 0, 0)]
    all_gather x1, waiting for transfers between devices: 128 us -> 43.3 us  [per_device(): lax.all_gather(value_states, 'ctx', axis=0, tiled=True)]
    all_to_all x0 -> x1, starting transfers between devices: none -> 15.4 us  [per_device(): lax.all_to_all(jnp.stack([key_states] * lax.axis_size('ctx')), 'ctx', 0, 0)]
    another operation x0 -> x2, local copies, waits for them, and re-layouts: none -> 10.2 us  [the longest x1 6.9 us: per_device(): key_part = jnp.concatenate(lax.all_to_all(jnp.stack([key_states] * lax.ax...]
    reshape x1 -> x0, local copies, waits for them, and re-layouts: 6.89 us -> none  [per_device(): lax.all_gather(key_states, 'ctx', axis=0, tiled=True)]
where the time goes in v1:
time: 275 us; the launch traced here: 274 us
  waiting for transfers between devices  167 us (61%)
  matrix products  37.7 us (14%)
  other arithmetic  22.3 us (8%)
  local copies, waits for them, and re-layouts  17.7 us (6%)
  starting transfers between devices  15.5 us (6%)
  between operations  13.5 us (5%)
    all_to_all x1, waiting for transfers between devices, per_device(): lax.all_to_all(jnp.stack([key_states] * lax.axis_size('ctx')), 'ctx', 0, 0)  99.9 us
    all_gather x1, waiting for transfers between devices, per_device(): lax.all_gather(value_states, 'ctx', axis=0, tiled=True)  43.3 us
    reduce_scatter x1, waiting for transfers between devices, per_device(): lax.psum_scatter(jnp.dot(attended, out_weight, preferred_element_type=jnp...  23.3 us
    dot_general x1, matrix products, online_update(): jnp.einsum('thgj,jhd->thgd', weights.astype(jnp.bfloat16), value_part, pr...  16.3 us
    dot_general x1, matrix products, online_update(): jnp.einsum('thgd,jhd->thgj', query_heads, key_part, preferred_element_typ...  15.7 us
    all_to_all x1, starting transfers between devices, per_device(): lax.all_to_all(jnp.stack([key_states] * lax.axis_size('ctx')), 'ctx', 0, 0)  15.4 us
    reduce_sum x1, other arithmetic, online_update(): row_total = jnp.sum(weights, axis=-1)  14.3 us
    another operation x1, local copies, waits for them, and re-layouts, per_device(): key_part = jnp.concatenate(lax.all_to_all(jnp.stack([key_states] * lax.ax...  6.9 us
  transfers between devices with their start and end apart: 3, of which 3 were waited for; matrix products, arithmetic and copies ran while one was open for 0% of the time, Pallas kernels for 0%

profile of v1, /device:TPU:1, one launch (start us, length us, event | category | flops | bytes accessed | tf_op | source)
XLA Modules:
  0.0 273.8 jit_solution(11058487967578582545)
XLA Ops:
  6.5 0.0 copy-start.1
  6.5 0.0 copy-start.2
  6.5 0.0 copy-start.3
  6.5 0.0 copy-start
  6.5 3.3 %stack.2 = bf16[64,128,256]{2,1,0:T(8,128)(2,1)} broadcast(bf16[128,256]{1,0:T(8,128)(2,1)} %param.10), dimensions={1,2} | broadcast | bytes 4259840 | tf_op jit(solution)/shard_map/stack | solution.py:56
  9.9 15.4 %all-to-all-start = ((bf16[64,128,256]{2,1,0:T(8,128)(2,1)}), bf16[64,128,256]{2,1,0:T(8,128)(2,1)}, u32[]{:S(2)}, u32[]{:S(2)}) async-start(bf16[64,128,256]{2,1,0:T(8,128)(2,1)} %stack.2), calls=%async_computation | async-start | bytes 8388608 | tf_op jit(solution)/shard_map/all_to_all | solution.py:56
  25.3 0.0 all-gather.2.cloned.1.call-start
  25.3 0.7 all-gather.2.cloned.1.call-update
  26.0 0.0 reduce-scatter.2.cloned.1.call-start
  26.1 99.9 %all-to-all-done = bf16[64,128,256]{2,1,0:T(8,128)(2,1)} async-done(((bf16[64,128,256]{2,1,0:T(8,128)(2,1)}), bf16[64,128,256]{2,1,0:T(8,128)(2,1)}, u32[]{:S(2)}, u32[]{:S(2)}) %all-to-all-start) | async-done | bytes 4194336 | tf_op jit(solution)/shard_map/all_to_all | solution.py:56
  125.9 43.3 %all-gather.2.cloned.1.call-done = bf16[8192,256]{1,0:T(8,128)(2,1)} async-done(((bf16[128,256]{1,0:T(8,128)(2,1)}), bf16[8192,256]{1,0:T(8,128)(2,1)}) %all-gather.2.cloned.1.call-update) | async-done | bytes 4194320 | tf_op jit(solution)/shard_map/all_gather | solution.py:58
  169.2 0.0 copy-done.1
  169.2 0.0 copy-done.2
  169.2 0.0 copy-done.3
  169.2 0.0 copy-done
  169.2 68.7 %conditional.1 = (f32[128,2,4]{0,2,1:T(4,128)S(1)}, f32[128,2,4,128]{0,3,2,1:T(8,128)S(1)}) conditional(s32[]{:T(128)} %convert_element_type.15, () %tuple.22, (s32[8192]{0:T(1024)S(1)}, s32[8192]{0:T(1024)S(1)}, s32[]{:T(128)}, s32[128]{0:T(128)S(1)}, s32[]{:T(128)}, /*index=5*/s32[8]{0:T(128)S(1)}, s32[8192]{0:T(1024)S(1)}, s32[8]{0:T(128)S(1)}, ...), branch_computations={%region_0.0_spmd, %region_1.4_spmd} | conditional | flops 4395662336 | bytes 147220624 | solution.py:76
  169.3 0.1 dynamic-slice_compare_fusion
  169.3 0.1 dynamic_slice.19
  169.4 0.1 compare_or_fusion
  169.5 0.1 dynamic_slice.20
  169.6 1.2 broadcast_subtract_fusion
  170.8 3.7 %broadcast_compare_fusion = pred[128,8192]{0,1:T(8,128)(4,1)S(1)} fusion(s32[128]{0:T(128)S(1)} %broadcast_add_fusion, s32[8192]{0:T(1024)S(1)} %get-tuple-element.121), kind=kLoop, calls=%fused_computation.14 | loop fusion | flops 1048576 | bytes 1081856 | tf_op jit(solution)/shard_map/cond/branch_1_fun/le | solution.py:66
  174.6 2.8 %or_and_fusion = pred[128,2,8192]{0,2,1:T(8,128)(4,1)S(1)} fusion(s32[128,8192]{0,1:T(8,128)S(1)} %broadcast_subtract_fusion, s32[2]{0:T(128)S(1)} %dynamic_slice.20, pred[2,8192]{1,0:T(4,128)(4,1)S(1)} %compare_or_fusion, pred[128,8192]{0,1:T(8,128)(4,1)S(1)} %broadcast_compare_fusion), kind=kLoop, calls=%fused_computation.9 | loop fusion | flops 6291456 | bytes 7356424 | tf_op jit(solution)/shard_map/cond/branch_1_fun/and | solution.py:66
  177.4 6.9 %reshape_reshape.6 = bf16[8192,2,128]{2,1,0:T(2,128)(2,1)} reshape(bf16[64,128,256]{2,1,0:T(8,128)(2,1)} %get-tuple-element.125) | data formatting | bytes 8388608 | tf_op jit(solution)/shard_map/reshape;reshape | solution.py:57
  184.3 0.2 reshape.121
  184.5 15.7 %fusion = (f32[128,2,4]{0,2,1:T(4,128)S(1)}, f32[2,8192,128,4]{2,1,3,0:T(8,128)}) fusion(pred[128,2,8192]{0,2,1:T(8,128)(4,1)S(1)} %or_and_fusion, bf16[128,2,4,128]{3,2,1,0:T(4,128)(2,1)S(1)} %reshape.121, bf16[8192,2,128,1]{2,1,0,3:T(2,128)(2,1)} %bitcast.23), kind=kOutput, calls=%fused_computation.2 | convolution fusion | flops 2172648448 | bytes 40112128 | tf_op jit(solution)/shard_map/cond/branch_1_fun/thgd,jhd->thgj/dot_general | solution.py:13
  200.2 6.9 %reshape.122 = bf16[8192,2,128]{2,1,0:T(2,128)(2,1)} reshape(bf16[8192,256]{1,0:T(8,128)(2,1)} %get-tuple-element.127) | data formatting | bytes 8388608 | tf_op jit(solution)/shard_map/reshape | solution.py:58
  207.1 16.3 %fusion.11 = f32[128,2,4,128]{3,0,2,1:T(8,128)S(1)} fusion(bf16[8192,2,128,1]{2,1,0,3:T(2,128)(2,1)} %bitcast.24, f32[2,8192,128,4]{2,1,3,0:T(8,128)} %get-tuple-element.142, f32[128,2,4]{0,2,1:T(4,128)S(1)} %broadcast_maximum_fusion, pred[128,2,8192]{0,2,1:T(8,128)(4,1)S(1)} %or_and_fusion), kind=kOutput, calls=%fused_computation.15 | convolution fusion | flops 2181038080 | bytes 40374272 | tf_op jit(solution)/shard_map/cond/branch_1_fun/thgj,jhd->thgd/dot_general | solution.py:21
  223.4 0.2 copy.36
  223.6 14.3 %fusion.4 = f32[128,2,4]{0,2,1:T(4,128)S(1)} fusion(f32[2,8192,128,4]{2,1,3,0:T(8,128)} %get-tuple-element.142, f32[128,2,4]{0,2,1:T(4,128)S(1)} %broadcast_maximum_fusion, pred[128,2,8192]{0,2,1:T(8,128)(4,1)S(1)} %or_and_fusion), kind=kLoop, calls=%fused_computation.6 | loop fusion | flops 33553408 | bytes 35659776 | tf_op jit(solution)/shard_map/cond/branch_1_fun/reduce_sum | solution.py:20
  237.9 0.1 divide_convert_fusion
  238.0 5.6 %convolution_convert_fusion = bf16[128,4096]{1,0:T(8,128)(2,1)} fusion(bf16[128,1024]{0,1:T(8,128)(2,1)S(1)} %bitcast.25, bf16[1024,4096]{1,0:T(8,128)(2,1)} %param.12), kind=kOutput, calls=%fused_computation.23 | convolution fusion | flops 1074266112 | bytes 9699328 | tf_op jit(solution)/shard_map/dot_general | solution.py:81
  243.6 0.0 reduce-scatter.2.cloned.1.call-update
  243.7 23.3 %reduce-scatter.2.cloned.1.call-done = bf16[32,4096]{1,0:T(8,128)(2,1)} async-done(((bf16[128,4096]{1,0:T(8,128)(2,1)}), bf16[32,4096]{1,0:T(8,128)(2,1)}) %reduce-scatter.2.cloned.1.call-update) | async-done | bytes 262160 | tf_op jit(solution)/shard_map/reduce_scatter | solution.py:80
  (4 shorter events, 0.0 us)
Async XLA Ops:
  6.5 162.7 %copy-start.1 = (s32[8]{0:T(128)S(1)}, s32[8]{0:T(128)}, u32[]{:S(2)}) copy-start(s32[8]{0:T(128)} %param.13) | copy-start | bytes 100
  6.5 162.7 %copy-start.2 = (s32[8]{0:T(128)S(1)}, s32[8]{0:T(128)}, u32[]{:S(2)}) copy-start(s32[8]{0:T(128)} %param.14) | copy-start | bytes 100
  6.5 162.7 %copy-start.3 = (s32[8]{0:T(128)S(1)}, s32[8]{0:T(128)}, u32[]{:S(2)}) copy-start(s32[8]{0:T(128)} %param.15) | copy-start | bytes 100
  6.5 162.7 %copy-start = (bf16[128,1024]{1,0:T(8,128)(2,1)S(1)}, bf16[128,1024]{1,0:T(8,128)(2,1)}, u32[]{:S(2)}) copy-start(bf16[128,1024]{1,0:T(8,128)(2,1)} %param.9) | copy-start | bytes 786436
  9.9 116.0 %all-to-all-start = ((bf16[64,128,256]{2,1,0:T(8,128)(2,1)}), bf16[64,128,256]{2,1,0:T(8,128)(2,1)}, u32[]{:S(2)}, u32[]{:S(2)}) async-start(bf16[64,128,256]{2,1,0:T(8,128)(2,1)} %stack.2), calls=%async_computation | async-start | bytes 8388608 | tf_op jit(solution)/shard_map/all_to_all | solution.py:56
  25.3 143.9 %all-gather.2.cloned.1.call-start = ((), (), s32[]{:S(2)}) async-start(), calls=%async_computation.2 | async-start | bytes 4259840 | tf_op jit(solution)/shard_map/all_gather | solution.py:58
  26.0 241.0 %reduce-scatter.2.cloned.1.call-start = ((), (), s32[]{:S(2)}) async-start(), calls=%async_computation.3 | async-start | bytes 1310720 | tf_op jit(solution)/shard_map/reduce_scatter | solution.py:80
Sparse Core Ops, SparseCore 0:
  29.6 139.5 all-gather.1
  243.8 23.1 reduce-scatter.1
